TPU v7x, 32 devices: a whole 2x2x4 slice. The times are simulated.
32 devices in a mesh: groups: 2 (over y), item: 4 (over z), dp: 2 (over core), tensor: 2 (over x).
Axes of the slice: x: 2, y: 2, z: 4, core: 2. Of those that a mesh axis runs over, the one named last changes fastest.
Arguments:
- events: bfloat16 [12288, 1024], P(('groups', 'item', 'dp')), parts along dimension 0, may hold values from -6 to 6
- lengths: int32 [16], P('groups'), parts along dimension 0, may hold values from 192 to 768, as said below
- packing: int32 [16], P('groups'), parts along dimension 0, may hold values from 0 to 7, each once
- positions: int32 [16, 64], P('groups'), parts along dimension 0, may hold values from 0 to 767, as said below
- logged: int32 [16, 64], P('groups'), parts along dimension 0, may hold values from 0 to 16383
- w_uvqk: bfloat16 [1024, 1024], P(None, 'tensor'), may hold values from -0.1875 to 0.1875
- w_out: bfloat16 [256, 1024], P('tensor'), may hold values from -0.375 to 0.375
- catalogue: bfloat16 [16384, 1024], P(('item', 'dp', 'tensor')), may hold values from -0.46875 to 0.46875
Outputs:
- scoring_state: bfloat16 [1024, 1024], P(('groups', 'item', 'dp'), 'tensor'), parts along dimension 0
- log_propensity: float32 [1024], P(('groups', 'item', 'dp')), parts along dimension 0
There are 2 independent parts, one for each index of `groups`. A program takes and returns all parts, laid end to end along the dimension named above; an argument that names none is the same for every part. Nothing has to cross between parts.
Inputs may be any that keep to these rules, and one draw needn't show every extreme that they name: `lengths`: one history has exactly 768 valid events and one exactly 192. positions[h, k] < lengths[h]. `packing`: each history id appears once.
All inputs are finite; a program needn't handle non-finite values.
Results may differ from a plain program's by a relative error of at most 0.0048.
Values may be sent and summed in bfloat16 or wider, within the bound.
A program may use at most 64 MiB of HBM per device.

v0:
```python
import math
import jax
import jax.numpy as jnp
from jax import lax
from jax.sharding import PartitionSpec as P

DH = 128


def pick_target(logits, item_ids, item_base):
    local_ids = item_ids - item_base
    matches = jnp.arange(logits.shape[1], dtype=jnp.int32)[None, :] == local_ids[:, None]
    return jnp.sum(jnp.where(matches, logits, 0.0), axis=1)


def local(events, lengths, packing, positions, logged, w_uvqk, w_out, catalogue):
    slot_rows, model_width = events.shape
    hist_count = packing.shape[0]
    imp_count = positions.shape[1]
    local_heads = w_out.shape[0] // DH
    item_count = catalogue.shape[0]
    slot_index = lax.axis_index(("item", "dp"))
    hist_ids = jnp.arange(hist_count, dtype=jnp.int32)
    slot_pick = (packing[:, None] == hist_ids[None, :]).astype(jnp.int32)
    owned = (hist_ids == slot_index).astype(jnp.int32)
    hist_row = jnp.sum(slot_pick * owned[:, None], axis=0)
    hist_length = jnp.sum(hist_row * lengths)
    event_spots = jnp.sum(hist_row[:, None] * positions, axis=0)
    slot_items = jnp.sum(slot_pick[:, :, None] * logged[None, :, :], axis=1).reshape(
        hist_count * imp_count
    )
    item_base = lax.axis_index(("item", "dp", "tensor")) * item_count
    split_weights = w_uvqk.reshape(model_width, local_heads, 4, DH)
    w_values_keys = split_weights[:, :, 1::2].reshape(model_width, local_heads * 2 * DH)
    w_gate_query = split_weights[:, :, 0::2].reshape(model_width, local_heads * 2 * DH)
    values_keys = jnp.dot(events, w_values_keys, preferred_element_type=jnp.float32)
    values_keys = (
        jax.nn.silu(values_keys).astype(jnp.bfloat16).reshape(slot_rows, local_heads, 2, DH)
    )
    chosen = jnp.take(events, event_spots, axis=0)
    gate_query = jnp.dot(chosen, w_gate_query, preferred_element_type=jnp.float32)
    gate_query = jax.nn.silu(gate_query).astype(jnp.bfloat16).reshape(imp_count, local_heads, 2, DH)
    scores = jnp.einsum(
        "ied,med->iem",
        gate_query[:, :, 1],
        values_keys[:, :, 1],
        preferred_element_type=jnp.float32,
    ) / math.sqrt(DH)
    slot_range = jnp.arange(slot_rows, dtype=jnp.int32)
    is_valid = (slot_range[None, :] <= event_spots[:, None]) & (slot_range[None, :] < hist_length)
    weights = jnp.where(is_valid[:, None, :], jax.nn.silu(scores), 0.0).astype(jnp.bfloat16)
    attended = jnp.einsum(
        "iem,med->ied", weights, values_keys[:, :, 0], preferred_element_type=jnp.float32
    )
    inverse = lax.rsqrt(jnp.mean(attended * attended, axis=-1, keepdims=True) + 1e-06)
    gated_rows = (attended * inverse * gate_query[:, :, 0].astype(jnp.float32)).astype(jnp.bfloat16)
    gated_rows = gated_rows.reshape(imp_count, local_heads * DH)
    partial_out = jnp.dot(gated_rows, w_out, preferred_element_type=jnp.float32)
    residual = chosen.astype(jnp.float32)
    col_share = model_width // lax.axis_size("tensor")
    col_start = lax.axis_index("tensor") * col_share
    summed = lax.psum(partial_out, "tensor")
    hidden_state = (summed + residual).astype(jnp.bfloat16)
    state_out = lax.dynamic_slice_in_dim(hidden_state, col_start, col_share, 1)
    logits = lax.dot_general(
        lax.all_gather(hidden_state, ("item", "dp"), axis=0, tiled=True),
        catalogue,
        (((1,), (1,)), ((), ())),
        preferred_element_type=jnp.float32,
    )
    new_totals = jnp.sum(jnp.exp(logits), axis=1)
    new_target = pick_target(logits, slot_items, item_base)
    whole_totals, whole_target = lax.psum((new_totals, new_target), ("item", "dp", "tensor"))
    mine_totals = lax.dynamic_slice_in_dim(whole_totals, slot_index * imp_count, imp_count, 0)
    mine_target = lax.dynamic_slice_in_dim(whole_target, slot_index * imp_count, imp_count, 0)
    return (state_out, mine_target - jnp.log(mine_totals))


def solution(mesh):
    placed = (
        P(("groups", "item", "dp"), None),
        P("groups"),
        P("groups"),
        P("groups", None),
        P("groups", None),
        P(None, "tensor"),
        P("tensor", None),
        P(("item", "dp", "tensor"), None),
    )
    return jax.shard_map(
        local,
        mesh=mesh,
        in_specs=placed,
        out_specs=(P(("groups", "item", "dp"), "tensor"), P(("groups", "item", "dp"))),
        check_vma=False,
    )
```

profile of v0, /device:TPU:0, one launch (start us, length us, event | category | flops | bytes accessed | tf_op | source)
XLA Modules:
  0.0 136.1 jit_solution(11309855949234600494)
XLA Ops:
  7.2 0.0 copy-start
  7.2 0.0 all-reduce.3.cloned.1.call-start
  7.2 0.9 select_reduce_fusion.1
  8.1 0.8 multiply_reduce_fusion.2
  8.9 1.3 reshape.175
  10.3 0.0 copy-start.5
  10.3 12.4 %slice.21 = bf16[1024,1,2,128]{3,2,0,1:T(2,128)(2,1)} slice(bf16[1024,1,4,128]{3,2,0,1:T(4,128)(2,1)S(1)} %reshape.175), slice={[0:1024:1], [0:1:1], [0:4:2], [0:128:1]} | slice | bytes 1048576 | tf_op jit(solution)/shard_map/slice | solution.py:35
  22.6 12.4 %slice.18 = bf16[1024,1,2,128]{3,2,0,1:T(2,128)(2,1)} slice(bf16[1024,1,4,128]{3,2,0,1:T(4,128)(2,1)S(1)} %reshape.175), slice={[0:1024:1], [0:1:1], [1:4:2], [0:128:1]} | slice | bytes 1048576 | tf_op jit(solution)/shard_map/slice | solution.py:34
  35.0 0.0 copy-start.1
  35.0 2.5 %gather_fusion = bf16[64,1024]{1,0:T(8,128)(2,1)S(1)} fusion(bf16[768,1024]{1,0:T(8,128)(2,1)} %param.8, s32[1024]{0:T(1024)S(1)} %pad_clamp_fusion), kind=kCustom, calls=%fused_computation | custom fusion | bytes 262400 | tf_op jit(solution)/shard_map/jit(_take)/gather | solution.py:40
  37.5 1.3 multiply_convert_fusion.1
  38.8 0.1 fusion.30
  38.9 0.0 copy-done.5
  38.9 0.6 multiply_reduce_fusion.3
  39.5 0.6 iota_compare_fusion.2
  40.2 0.0 copy-done.1
  40.2 0.0 copy-start.2
  40.2 2.1 %multiply_convert_fusion = bf16[768,256]{0,1:T(8,128)(2,1)S(1)} fusion(bf16[768,1024]{1,0:T(8,128)(2,1)} %param.8, bf16[128,8,2,128]{3,2,1,0:T(2,128)(2,1)S(1)} %bitcast.81), kind=kOutput, calls=%fused_computation.7 | convolution fusion | flops 403636224 | bytes 2490368 | tf_op jit(solution)/shard_map/dot_general | solution.py:36
  42.4 0.0 copy-start.4
  42.4 0.0 copy-start.3
  42.4 0.4 multiply_reduce_fusion.1
  42.8 0.0 copy-done.2
  42.8 0.9 fusion.21
  43.8 0.0 all-reduce.3.cloned.1.call-update
  43.8 0.0 all-gather.2.cloned.1.call-start
  43.9 26.0 %all-reduce.3.cloned.1.call-done = f32[64,1024]{1,0:T(8,128)} async-done(((f32[64,1024]{1,0:T(8,128)}), f32[64,1024]{1,0:T(8,128)}) %all-reduce.3.cloned.1.call-update) | async-done | bytes 262160 | tf_op jit(solution)/shard_map/psum | solution.py:62
  69.8 1.7 %add_convert_fusion = bf16[64,1024]{1,0:T(8,128)(2,1)} fusion(f32[64,1024]{1,0:T(8,128)} %all-reduce.3.cloned.1.call-done, bf16[64,1024]{1,0:T(8,128)(2,1)S(1)} %gather_fusion, pred[64]{0:T(512)(128)(4,1)S(1)} %compare_and_fusion), kind=kLoop, calls=%fused_computation.14 | loop fusion | flops 262144 | bytes 524352 | tf_op jit(solution)/shard_map/convert_element_type | solution.py:63
  71.5 0.0 all-gather.2.cloned.1.call-update
  71.6 0.0 copy-done.4
  71.6 0.1 fusion.24
  71.6 0.0 copy-done.3
  71.7 0.1 multiply_reduce_fusion
  71.8 0.1 sub.18
  71.8 1.5 %constant_dynamic-slice_fusion = bf16[64,512]{1,0:T(8,128)(2,1)} fusion(bf16[64,1024]{1,0:T(8,128)(2,1)} %add_convert_fusion, s32[]{:T(128)S(6)} %select_n.39), kind=kLoop, calls=%fused_computation.52 | loop fusion | bytes 131076 | tf_op jit(solution)/shard_map/dynamic_slice | solution.py:64
  73.3 20.5 %all-gather.2.cloned.1.call-done = bf16[512,1024]{1,0:T(8,128)(2,1)} async-done(((bf16[64,1024]{1,0:T(8,128)(2,1)}), bf16[512,1024]{1,0:T(8,128)(2,1)}) %all-gather.2.cloned.1.call-update) | async-done | bytes 1048592 | tf_op jit(solution)/shard_map/all_gather | solution.py:66
  93.8 0.0 copy-done
  93.8 2.8 %select_reduce_fusion = (f32[512]{0:T(512)S(1)}, f32[512]{0:T(512)S(1)}) fusion(s32[512]{0:T(512)S(1)} %sub.18, bf16[512,1024]{1,0:T(8,128)(2,1)} %all-gather.2.cloned.1.call-done, bf16[1024,1024]{1,0:T(8,128)(2,1)S(1)} %copy-done), kind=kOutput, calls=%fused_computation.2 | convolution fusion | flops 1075837952 | bytes 3151872 | tf_op jit(solution)/shard_map/dot_general | solution.py:65
  96.6 32.1 %all-reduce = (f32[512]{0:T(512)S(1)}, f32[512]{0:T(512)S(1)}) all-reduce(f32[512]{0:T(512)S(1)} %get-tuple-element.3, f32[512]{0:T(512)S(1)} %get-tuple-element.2), channel_id=1, replica_groups=mesh['groups'=2,'item'=4,'dp'=2,'tensor'=2] {'item','dp','tensor'}, use_global_device_ids=true, to_apply=%region_9.10 | all-reduce | flops 1024 | bytes 8192 | tf_op jit(solution)/shard_map/psum | solution.py:73
  128.7 0.6 log_subtract_fusion
  (7 shorter events, 0.1 us)
Async XLA Ops:
  7.2 86.7 %copy-start = (bf16[1024,1024]{1,0:T(8,128)(2,1)S(1)}, bf16[1024,1024]{1,0:T(8,128)(2,1)}, u32[]{:S(2)}) copy-start(bf16[1024,1024]{1,0:T(8,128)(2,1)} %param.15) | copy-start | bytes 6291460
  7.2 62.7 %all-reduce.3.cloned.1.call-start = ((), (), s32[]{:S(2)}) async-start(), calls=%async_computation | async-start | bytes 524288 | tf_op jit(solution)/shard_map/psum | solution.py:62
  10.3 28.6 %copy-start.5 = (s32[8]{0:T(128)S(1)}, s32[8]{0:T(128)}, u32[]{:S(2)}) copy-start(s32[8]{0:T(128)} %param.9) | copy-start | bytes 100
  35.0 5.2 %copy-start.1 = (bf16[1024,1,2,128]{3,2,0,1:T(2,128)(2,1)S(1)}, bf16[1024,1,2,128]{3,2,0,1:T(2,128)(2,1)}, u32[]{:S(2)}) copy-start(bf16[1024,1,2,128]{3,2,0,1:T(2,128)(2,1)} %slice.18) | copy-start | bytes 1572868
  40.2 2.6 %copy-start.2 = (bf16[128,1024]{1,0:T(8,128)(2,1)S(1)}, bf16[128,1024]{1,0:T(8,128)(2,1)}, u32[]{:S(2)}) copy-start(bf16[128,1024]{1,0:T(8,128)(2,1)} %param.14) | copy-start | bytes 786436
  42.4 29.2 %copy-start.4 = (s32[8]{0:T(128)S(1)}, s32[8]{0:T(128)}, u32[]{:S(2)}) copy-start(s32[8]{0:T(128)} %param.10) | copy-start | bytes 100
  42.4 29.3 %copy-start.3 = (s32[8,64]{1,0:T(8,128)S(1)}, s32[8,64]{1,0:T(8,128)}, u32[]{:S(2)}) copy-start(s32[8,64]{1,0:T(8,128)} %param.12) | copy-start | bytes 6148
  43.8 50.0 %all-gather.2.cloned.1.call-start = ((), (), s32[]{:S(2)}) async-start(), calls=%async_computation.1 | async-start | bytes 1179648 | tf_op jit(solution)/shard_map/all_gather | solution.py:66
Sparse Core Ops, SparseCore 0:
  43.9 25.8 all-reduce.2
  71.7 22.0 all-gather.1
where the time goes:
time: 137 us; the launch traced here: 136 us
  waiting for transfers between devices  46.5 us (34%)
  blocking collectives  32.1 us (23%)
  local copies, waits for them, and re-layouts  30.2 us (22%)
  between operations  14.2 us (10%)
  matrix products  7.63 us (6%)
  other arithmetic  5.41 us (4%)
    psum x1, blocking collectives, local(): lax.psum((new_totals, new_target), ('item', 'dp', 'tensor'))  32.1 us
    psum x1, waiting for transfers between devices, local(): summed = lax.psum(partial_out, 'tensor')  26 us
    all_gather x1, waiting for transfers between devices, local(): lax.all_gather(hidden_state, ('item', 'dp'), axis=0, tiled=True)  20.5 us
    slice x1, local copies, waits for them, and re-layouts, local(): split_weights[:, :, 1::2].reshape(model_width, local_heads * 2 * DH)  12.4 us
    slice x1, local copies, waits for them, and re-layouts, local(): split_weights[:, :, 0::2].reshape(model_width, local_heads * 2 * DH)  12.4 us
    dot_general x1, matrix products, local(): lax.dot_general(lax.all_gather(hidden_state, ('item', 'dp'), axis=0, tile...  2.82 us
  transfers between devices with their start and end apart: 2, of which 2 were waited for; matrix products, arithmetic and copies ran while one was open for 1% of the time, Pallas kernels for 0%

commit v1 on v0

--- a/solution.py
+++ b/solution.py
@@ -59,7 +59,7 @@
     residual = chosen.astype(jnp.float32)
     col_share = model_width // lax.axis_size("tensor")
     col_start = lax.axis_index("tensor") * col_share
-    summed = lax.psum(partial_out, "tensor")
+    summed = jnp.sum(lax.all_gather(partial_out, "tensor"), axis=0)
     hidden_state = (summed + residual).astype(jnp.bfloat16)
     state_out = lax.dynamic_slice_in_dim(hidden_state, col_start, col_share, 1)
     logits = lax.dot_general(

time: 137 us -> 120 us (0.88)
  waiting for transfers between devices: 46.5 us -> 22 us
  blocking collectives: 32.1 us -> 42 us
    psum x1 -> x0, waiting for transfers between devices: 26 us -> none  [local(): summed = lax.psum(partial_out, 'tensor')]
    all_gather x0 -> x1, blocking collectives: none -> 9.91 us  [local(): summed = jnp.sum(lax.all_gather(partial_out, 'tensor'), axis=0)]
    all_gather x1, waiting for transfers between devices: 20.5 us -> 22 us  [local(): lax.all_gather(hidden_state, ('item', 'dp'), axis=0, tiled=True)]
  transfers between devices with their start and end apart: 2 -> 1, of which waited for: 2 -> 1; matrix products, arithmetic and copies ran while one was open for 1% -> 1% of each run, Pallas kernels for 0% -> 0%
where the time goes in v1:
time: 120 us
  blocking collectives  42 us (35%)
  local copies, waits for them, and re-layouts  30.2 us (25%)
  waiting for transfers between devices  22 us (18%)
  between operations  14.2 us (12%)
  matrix products  6.91 us (6%)
  other arithmetic  4.49 us (4%)
    psum x1, blocking collectives, local(): lax.psum((new_totals, new_target), ('item', 'dp', 'tensor'))  32.1 us
    all_gather x1, waiting for transfers between devices, local(): lax.all_gather(hidden_state, ('item', 'dp'), axis=0, tiled=True)  22 us
    slice x1, local copies, waits for them, and re-layouts, local(): split_weights[:, :, 1::2].reshape(model_width, local_heads * 2 * DH)  12.4 us
    slice x1, local copies, waits for them, and re-layouts, local(): split_weights[:, :, 0::2].reshape(model_width, local_heads * 2 * DH)  12.4 us
    all_gather x1, blocking collectives, local(): summed = jnp.sum(lax.all_gather(partial_out, 'tensor'), axis=0)  9.91 us
    dot_general x1, matrix products, local(): lax.dot_general(lax.all_gather(hidden_state, ('item', 'dp'), axis=0, tile...  2.81 us
    gather x1, local copies, waits for them, and re-layouts, local(): chosen = jnp.take(events, event_spots, axis=0)  2.47 us
  transfers between devices with their start and end apart: 1, of which 1 were waited for; matrix products, arithmetic and copies ran while one was open for 1% of the time, Pallas kernels for 0%

profile of v1, /device:TPU:0, one launch (start us, length us, event | category | flops | bytes accessed | tf_op | source)
XLA Modules:
  0.0 119.9 jit_solution(9270770067745469469)
XLA Ops:
  7.2 0.0 copy-start
  7.2 0.0 all-gather.3.cloned.1.call-start
  7.2 0.9 select_reduce_fusion.1
  8.1 0.8 multiply_reduce_fusion.2
  8.9 1.3 %reshape.175 = bf16[1024,1,4,128]{3,2,0,1:T(4,128)(2,1)S(1)} reshape(bf16[1024,512]{1,0:T(8,128)(2,1)} %param.13) | data formatting | bytes 2097152 | tf_op jit(solution)/shard_map/reshape | solution.py:33
  10.3 0.0 copy-start.5
  10.3 12.4 %slice.21 = bf16[1024,1,2,128]{3,2,0,1:T(2,128)(2,1)} slice(bf16[1024,1,4,128]{3,2,0,1:T(4,128)(2,1)S(1)} %reshape.175), slice={[0:1024:1], [0:1:1], [0:4:2], [0:128:1]} | slice | bytes 1048576 | tf_op jit(solution)/shard_map/slice | solution.py:35
  22.6 12.4 %slice.18 = bf16[1024,1,2,128]{3,2,0,1:T(2,128)(2,1)} slice(bf16[1024,1,4,128]{3,2,0,1:T(4,128)(2,1)S(1)} %reshape.175), slice={[0:1024:1], [0:1:1], [1:4:2], [0:128:1]} | slice | bytes 1048576 | tf_op jit(solution)/shard_map/slice | solution.py:34
  35.0 0.0 copy-start.1
  35.0 2.5 %gather_fusion = bf16[64,1024]{1,0:T(8,128)(2,1)S(1)} fusion(bf16[768,1024]{1,0:T(8,128)(2,1)} %param.8, s32[1024]{0:T(1024)S(1)} %pad_clamp_fusion), kind=kCustom, calls=%fused_computation | custom fusion | bytes 262400 | tf_op jit(solution)/shard_map/jit(_take)/gather | solution.py:40
  37.5 1.3 %multiply_convert_fusion.1 = bf16[64,256]{1,0:T(8,128)(2,1)S(1)} fusion(bf16[128,8,2,128]{3,2,1,0:T(2,128)(2,1)} %bitcast.84, bf16[64,1024]{1,0:T(8,128)(2,1)S(1)} %gather_fusion, pred[64]{0:T(512)(128)(4,1)S(1)} %compare_and_fusion), kind=kOutput, calls=%fused_computation.27 | convolution fusion | flops 33701888 | bytes 688192 | tf_op jit(solution)/shard_map/dot_general | solution.py:41
  38.8 0.1 fusion.30
  38.9 0.0 copy-done.5
  38.9 0.6 multiply_reduce_fusion.3
  39.5 0.6 iota_compare_fusion.2
  40.2 0.0 copy-done.1
  40.2 0.0 copy-start.2
  40.2 2.1 %multiply_convert_fusion = bf16[768,256]{0,1:T(8,128)(2,1)S(1)} fusion(bf16[768,1024]{1,0:T(8,128)(2,1)} %param.8, bf16[128,8,2,128]{3,2,1,0:T(2,128)(2,1)S(1)} %bitcast.83), kind=kOutput, calls=%fused_computation.7 | convolution fusion | flops 403636224 | bytes 2490368 | tf_op jit(solution)/shard_map/dot_general | solution.py:36
  42.4 0.0 copy-start.4
  42.4 0.0 copy-start.3
  42.4 0.4 multiply_reduce_fusion.1
  42.8 0.0 copy-done.2
  42.8 0.2 fusion.21
  43.1 9.9 %all-gather = f32[128,1024]{1,0:T(8,128)S(1)} all-gather(f32[64,1024]{1,0:T(8,128)S(1)} %fusion.21), channel_id=2, replica_groups=mesh['groups'=2,'item'=4,'dp'=2,'tensor'=2] {'tensor'}, dimensions={0}, use_global_device_ids=true | all-gather | bytes 786432 | tf_op jit(solution)/shard_map/all_gather | solution.py:62
  53.0 0.7 add_convert_fusion
  53.8 0.0 all-gather.3.cloned.1.call-update
  53.8 0.0 copy-done.4
  53.8 0.1 fusion.24
  53.9 0.0 copy-done.3
  53.9 0.1 multiply_reduce_fusion
  54.0 0.1 sub.18
  54.1 1.5 %constant_dynamic-slice_fusion = bf16[64,512]{1,0:T(8,128)(2,1)} fusion(bf16[64,1024]{1,0:T(8,128)(2,1)} %add_convert_fusion, s32[]{:T(128)S(6)} %select_n.39), kind=kLoop, calls=%fused_computation.52 | loop fusion | bytes 131076 | tf_op jit(solution)/shard_map/dynamic_slice | solution.py:64
  55.5 22.0 %all-gather.3.cloned.1.call-done = bf16[512,1024]{1,0:T(8,128)(2,1)} async-done(((bf16[64,1024]{1,0:T(8,128)(2,1)}), bf16[512,1024]{1,0:T(8,128)(2,1)}) %all-gather.3.cloned.1.call-update) | async-done | bytes 1048592 | tf_op jit(solution)/shard_map/all_gather | solution.py:66
  77.6 0.0 copy-done
  77.6 2.8 %select_reduce_fusion = (f32[512]{0:T(512)S(1)}, f32[512]{0:T(512)S(1)}) fusion(s32[512]{0:T(512)S(1)} %sub.18, bf16[512,1024]{1,0:T(8,128)(2,1)} %all-gather.3.cloned.1.call-done, bf16[1024,1024]{1,0:T(8,128)(2,1)S(1)} %copy-done), kind=kOutput, calls=%fused_computation.2 | convolution fusion | flops 1075837952 | bytes 3151872 | tf_op jit(solution)/shard_map/dot_general | solution.py:65
  80.4 32.1 %all-reduce = (f32[512]{0:T(512)S(1)}, f32[512]{0:T(512)S(1)}) all-reduce(f32[512]{0:T(512)S(1)} %get-tuple-element.3, f32[512]{0:T(512)S(1)} %get-tuple-element.2), channel_id=1, replica_groups=mesh['groups'=2,'item'=4,'dp'=2,'tensor'=2] {'item','dp','tensor'}, use_global_device_ids=true, to_apply=%region_9.10 | all-reduce | flops 1024 | bytes 8192 | tf_op jit(solution)/shard_map/psum | solution.py:73
  112.4 0.6 log_subtract_fusion
  (8 shorter events, 0.1 us)
Async XLA Ops:
  7.2 70.4 %copy-start = (bf16[1024,1024]{1,0:T(8,128)(2,1)S(1)}, bf16[1024,1024]{1,0:T(8,128)(2,1)}, u32[]{:S(2)}) copy-start(bf16[1024,1024]{1,0:T(8,128)(2,1)} %param.15) | copy-start | bytes 6291460
  7.2 70.4 %all-gather.3.cloned.1.call-start = ((), (), s32[]{:S(2)}) async-start(), calls=%async_computation | async-start | bytes 1179648 | tf_op jit(solution)/shard_map/all_gather | solution.py:66
  10.3 28.6 %copy-start.5 = (s32[8]{0:T(128)S(1)}, s32[8]{0:T(128)}, u32[]{:S(2)}) copy-start(s32[8]{0:T(128)} %param.9) | copy-start | bytes 100
  35.0 5.2 %copy-start.1 = (bf16[1024,1,2,128]{3,2,0,1:T(2,128)(2,1)S(1)}, bf16[1024,1,2,128]{3,2,0,1:T(2,128)(2,1)}, u32[]{:S(2)}) copy-start(bf16[1024,1,2,128]{3,2,0,1:T(2,128)(2,1)} %slice.18) | copy-start | bytes 1572868
  40.2 2.6 %copy-start.2 = (bf16[128,1024]{1,0:T(8,128)(2,1)S(1)}, bf16[128,1024]{1,0:T(8,128)(2,1)}, u32[]{:S(2)}) copy-start(bf16[128,1024]{1,0:T(8,128)(2,1)} %param.14) | copy-start | bytes 786436
  42.4 11.4 %copy-start.4 = (s32[8]{0:T(128)S(1)}, s32[8]{0:T(128)}, u32[]{:S(2)}) copy-start(s32[8]{0:T(128)} %param.10) | copy-start | bytes 100
  42.4 11.5 %copy-start.3 = (s32[8,64]{1,0:T(8,128)S(1)}, s32[8,64]{1,0:T(8,128)}, u32[]{:S(2)}) copy-start(s32[8,64]{1,0:T(8,128)} %param.12) | copy-start | bytes 6148
Sparse Core Ops, SparseCore 0:
  53.9 23.6 all-gather.2
